TPU v7x, 32 devices: a whole 2x2x4 slice. The times are simulated.
32 devices in a mesh: cell: 2 (over y), gene: 16 (over z, x, core).
Axes of the slice: x: 2, y: 2, z: 4, core: 2. Of those that a mesh axis runs over, the one named last changes fastest.
Arguments:
- blocks: bfloat16 [1536, 256, 256], P(('cell', 'gene')), may hold values from 0 to 255, as said below
- block_rows: int32 [1536], P(('cell', 'gene')), may hold values from 0 to 15, as said below
- block_cols: int32 [1536], P(('cell', 'gene')), may hold values from 0 to 3, as said below
- block_count: int32 [32], P(('cell', 'gene')), may hold values from 2 to 48, as said below
- cell_factor: float32 [8192, 128], P(('cell', 'gene')), as said below
- gene_factor: float32 [16384, 128], P('gene'), as said below
Outputs:
- cell_new: float32 [8192, 128], P(('cell', 'gene'))
- gene_new: float32 [16384, 128], P('gene')
Inputs may be any that keep to these rules, and one draw needn't show every extreme that they name: `blocks`: counts are whole numbers. `block_rows`: within one device the live slots and the padding slots name distinct block positions. `block_cols`: within one device the live slots and the padding slots name distinct block positions. `block_count`: some device has all 48 slots live. `cell_factor`: positive entries. `gene_factor`: positive entries.
All inputs are finite; a program needn't handle non-finite values.
Results may differ from a plain program's by a relative error of at most 0.00084.
Values may be sent and summed in bfloat16 or wider, within the bound.
A program may use at most 64 MiB of HBM per device.

v0:
```python
import jax
import jax.numpy as jnp
from jax import lax
from jax.sharding import PartitionSpec as P


def block_ratio(blocks, row_tiles, col_tiles, live):
    model = jnp.einsum("nir,njr->nij", row_tiles, col_tiles, preferred_element_type=jnp.float32)
    return (blocks.astype(jnp.float32) / model * live[:, None, None]).astype(jnp.bfloat16)


def on_device(blocks, block_rows, block_cols, block_count, cell_factor, gene_factor):
    slots = blocks.shape[0]
    width = blocks.shape[1]
    rank = cell_factor.shape[1]
    gene_len = gene_factor.shape[0]
    live = (jnp.arange(slots, dtype=jnp.int32) < block_count[0]).astype(jnp.float32)
    gene_bf = gene_factor.astype(jnp.bfloat16)
    gene_tiles = gene_bf.reshape(-1, width, rank)[block_cols]
    gene_totals = lax.psum(jnp.sum(gene_factor, 0), "gene")
    cell_full = lax.all_gather(cell_factor, "gene", axis=0, tiled=True)
    cell_bf = cell_full.astype(jnp.bfloat16)
    row_count = cell_bf.shape[0] // width
    row_pick = (block_rows[None, :] == jnp.arange(row_count, dtype=jnp.int32)[:, None]).astype(
        jnp.float32
    )
    col_pick = (
        block_cols[None, :] == jnp.arange(gene_len // width, dtype=jnp.int32)[:, None]
    ).astype(jnp.float32)
    row_tiles = cell_bf.reshape(row_count, width, rank)[block_rows]
    ratio = block_ratio(blocks, row_tiles, gene_tiles, live)
    terms = jnp.einsum("nij,njr->nir", ratio, gene_tiles, preferred_element_type=jnp.float32)
    numer = jnp.einsum("bn,nir->bir", row_pick, terms, precision=lax.Precision.HIGHEST).reshape(
        -1, rank
    )
    whole = lax.psum(numer, "gene")
    group_new = cell_full * whole / gene_totals
    new_bf = group_new.astype(jnp.bfloat16)
    cell_sums = lax.psum(jnp.sum(group_new, 0), "cell")
    own_rows = cell_factor.shape[0]
    cell_new = lax.dynamic_slice_in_dim(group_new, lax.axis_index("gene") * own_rows, own_rows, 0)
    new_tiles = new_bf.reshape(row_count, width, rank)[block_rows]
    ratio_next = block_ratio(blocks, new_tiles, gene_tiles, live)
    terms_next = jnp.einsum(
        "nij,nir->njr", ratio_next, new_tiles, preferred_element_type=jnp.float32
    )
    numer_gene = jnp.einsum(
        "bn,njr->bjr", col_pick, terms_next, precision=lax.Precision.HIGHEST
    ).reshape(-1, rank)
    total = lax.psum(numer_gene, "cell")
    gene_new = gene_factor * total / cell_sums
    return (cell_new, gene_new)


def solution(mesh):
    placed = (
        P(("cell", "gene"), None, None),
        P(("cell", "gene")),
        P(("cell", "gene")),
        P(("cell", "gene")),
        P(("cell", "gene"), None),
        P("gene", None),
    )
    return jax.shard_map(
        on_device,
        mesh=mesh,
        in_specs=placed,
        out_specs=(P(("cell", "gene"), None), P("gene", None)),
        check_vma=False,
    )
```

profile of v0, /device:TPU:0, one launch (start us, length us, event | category | flops | bytes accessed | tf_op | source)
XLA Modules:
  0.0 241.2 jit_solution(14404089688201856968)
XLA Ops:
  7.2 0.7 all-gather.2.cloned.1.call-update
  7.9 0.0 all-reduce.3.cloned.1.call-start
  8.6 0.7 compare_select_fusion
  9.3 1.4 fusion.23
  10.7 2.8 %gather_fusion.1 = bf16[48,256,128]{2,1,0:T(8,128)(2,1)} fusion(bf16[4,256,128]{2,1,0:T(8,128)(2,1)S(1)} %bitcast.19, s32[1024]{0:T(1024)S(1)} %pad_clamp_fusion), kind=kCustom, calls=%fused_computation.1 | custom fusion | bytes 6291648 | tf_op jit(solution)/shard_map/gather | solution.py:19
  13.5 40.9 %all-gather.2.cloned.1.call-done = f32[4096,128]{1,0:T(8,128)} async-done(((f32[256,128]{1,0:T(8,128)}), f32[4096,128]{1,0:T(8,128)}) %all-gather.2.cloned.1.call-update) | async-done | bytes 2097168 | tf_op jit(solution)/shard_map/all_gather | solution.py:21
  54.3 1.7 convert_element_type.29
  56.0 2.7 %gather_fusion = bf16[48,256,128]{2,1,0:T(8,128)(2,1)} fusion(bf16[16,256,128]{2,1,0:T(8,128)(2,1)S(1)} %bitcast.21, s32[1024]{0:T(1024)S(1)} %pad_clamp_fusion.1), kind=kCustom, calls=%fused_computation | custom fusion | bytes 6291648 | tf_op jit(solution)/shard_map/gather | solution.py:30
  58.7 11.7 %fusion.10 = f32[48,256,128]{2,1,0:T(8,128)} fusion(bf16[48,256,128]{2,1,0:T(8,128)(2,1)} %gather_fusion.1, bf16[48,256,256]{2,1,0:T(8,128)(2,1)} %param.6, f32[48]{0:T(128)S(1)} %compare_convert_fusion, bf16[48,256,128]{2,1,0:T(8,128)(2,1)} %gather_fusion), kind=kOutput, calls=%fused_computation.14 | convolution fusion | flops 1623195648 | bytes 18874560 | tf_op jit(solution)/shard_map/nij,njr->nir/dot_general | solution.py:32
  70.4 8.4 %fusion.6 = f32[16,256,128]{2,0,1:T(8,128)S(1)} fusion(f32[48,256,128]{2,1,0:T(8,128)} %fusion.10, s32[48]{0:T(128)S(1)} %copy-done.1), kind=kOutput, calls=%fused_computation.11 | convolution fusion | flops 301990656 | bytes 8388800 | tf_op jit(solution)/shard_map/bn,nir->bir/dot_general | solution.py:33
  78.8 2.0 copy.8
  80.8 0.0 all-reduce.5.cloned.1.call-start
  80.9 31.9 %psum.29 = f32[128]{0:T(128)S(1)} all-reduce(f32[128]{0:T(128)S(1)} %get-tuple-element.5), channel_id=1, replica_groups=mesh['cell'=2,'gene'=16] {'gene'}, use_global_device_ids=true, to_apply=%region_2.0 | all-reduce | flops 128 | bytes 1024 | tf_op jit(solution)/shard_map/psum | solution.py:20
  112.8 65.2 %all-reduce.3.cloned.1.call-done = f32[4096,128]{1,0:T(8,128)} async-done(((f32[4096,128]{1,0:T(8,128)}), f32[4096,128]{1,0:T(8,128)}) %all-reduce.3.cloned.1.call-update) | async-done | bytes 2097168 | tf_op jit(solution)/shard_map/psum | solution.py:36
  177.9 2.8 %fusion.22 = (f32[128]{0:T(128)S(1)}, f32[4096,128]{1,0:T(8,128)S(1)}) fusion(f32[128]{0:T(128)S(1)} %psum.29, f32[4096,128]{1,0:T(8,128)} %all-gather.2.cloned.1.call-done, f32[4096,128]{1,0:T(8,128)} %all-reduce.3.cloned.1.call-done), kind=kLoop, calls=%fused_computation.31 | loop fusion | flops 1572736 | bytes 6292480 | tf_op jit(solution)/shard_map/reduce_sum | solution.py:39
  180.7 0.1 convert_element_type.33
  180.8 2.7 %gather_fusion.2 = bf16[48,256,128]{2,1,0:T(8,128)(2,1)} fusion(bf16[16,256,128]{2,1,0:T(8,128)(2,1)S(1)} %bitcast.20, s32[1024]{0:T(1024)S(1)} %pad_clamp_fusion.1), kind=kCustom, calls=%fused_computation.2 | custom fusion | bytes 6291648 | tf_op jit(solution)/shard_map/gather | solution.py:42
  183.5 12.2 %fusion.8 = f32[48,256,128]{2,1,0:T(8,128)} fusion(bf16[48,256,128]{2,1,0:T(8,128)(2,1)} %gather_fusion.2, bf16[48,256,256]{2,1,0:T(8,128)(2,1)} %param.6, f32[48]{0:T(128)S(1)} %compare_convert_fusion, bf16[48,256,128]{2,1,0:T(8,128)(2,1)} %gather_fusion.1), kind=kOutput, calls=%fused_computation.13 | convolution fusion | flops 1623195648 | bytes 18874560 | tf_op jit(solution)/shard_map/nij,nir->njr/dot_general | solution.py:44
  195.7 8.2 %fusion.4 = f32[4,256,128]{2,0,1:T(4,128)S(1)} fusion(f32[48,256,128]{2,1,0:T(8,128)} %fusion.8, s32[48]{0:T(128)S(1)} %copy-done.2), kind=kOutput, calls=%fused_computation.9 | convolution fusion | flops 75497664 | bytes 6815936 | tf_op jit(solution)/shard_map/bn,njr->bjr/dot_general | solution.py:47
  203.9 0.8 copy.9
  204.7 4.9 %psum.31 = f32[128]{0:T(128)S(1)} all-reduce(f32[128]{0:T(128)S(1)} %get-tuple-element.2), channel_id=1, replica_groups=mesh['cell'=2,'gene'=16] {'cell'}, use_global_device_ids=true, to_apply=%region_5.0 | all-reduce | flops 128 | bytes 1024 | tf_op jit(solution)/shard_map/psum | solution.py:39
  209.7 0.7 constant_dynamic-slice_fusion
  210.3 22.5 %all-reduce.5.cloned.1.call-done = f32[1024,128]{1,0:T(8,128)} async-done(((f32[1024,128]{1,0:T(8,128)}), f32[1024,128]{1,0:T(8,128)}) %all-reduce.5.cloned.1.call-update) | async-done | bytes 524304 | tf_op jit(solution)/shard_map/psum | solution.py:50
  232.8 1.9 multiply_divide_fusion.1
  (13 shorter events, 0.1 us)
Async XLA Ops:
  7.2 47.2 %all-gather.2.cloned.1.call-start = ((), (), s32[]{:S(2)}) async-start(), calls=%async_computation | async-start | bytes 2228224 | tf_op jit(solution)/shard_map/all_gather | solution.py:21
  7.9 170.0 %all-reduce.3.cloned.1.call-start = ((), (), s32[]{:S(2)}) async-start(), calls=%async_computation.1 | async-start | bytes 4194304 | tf_op jit(solution)/shard_map/psum | solution.py:36
  10.7 2.8 %copy-start.1 = (s32[48]{0:T(128)S(1)}, s32[48]{0:T(128)}, u32[]{:S(2)}) copy-start(s32[48]{0:T(128)} %param.7) | copy-start | bytes 580
  80.8 152.0 %all-reduce.5.cloned.1.call-start = ((), (), s32[]{:S(2)}) async-start(), calls=%async_computation.2 | async-start | bytes 1048576 | tf_op jit(solution)/shard_map/psum | solution.py:50
  183.5 12.2 %copy-start.2 = (s32[48]{0:T(128)S(1)}, s32[48]{0:T(128)}, u32[]{:S(2)}) copy-start(s32[48]{0:T(128)} %param.8) | copy-start | bytes 580
  195.7 37.1 %copy-start = (f32[1024,128]{1,0:T(8,128)S(1)}, f32[1024,128]{1,0:T(8,128)}, u32[]{:S(2)}) copy-start(f32[1024,128]{1,0:T(8,128)} %param.11) | copy-start | bytes 1572868
Sparse Core Ops, SparseCore 0:
  10.1 44.1 all-gather.1
  80.9 96.9 all-reduce.2
  204.9 27.9 all-reduce.4
where the time goes:
time: 242 us; the launch traced here: 241 us
  waiting for transfers between devices  129 us (53%)
  matrix products  40.5 us (17%)
  blocking collectives  36.8 us (15%)
  between operations  14.4 us (6%)
  local copies, waits for them, and re-layouts  11.6 us (5%)
  other arithmetic  8.57 us (4%)
    psum x1, waiting for transfers between devices, on_device(): whole = lax.psum(numer, 'gene')  65.2 us
    all_gather x1, waiting for transfers between devices, on_device(): cell_full = lax.all_gather(cell_factor, 'gene', axis=0, tiled=True)  40.9 us
    psum x1, blocking collectives, on_device(): gene_totals = lax.psum(jnp.sum(gene_factor, 0), 'gene')  31.9 us
    psum x1, waiting for transfers between devices, on_device(): total = lax.psum(numer_gene, 'cell')  22.5 us
    dot_general x1, matrix products, on_device(): jnp.einsum('nij,nir->njr', ratio_next, new_tiles, preferred_element_type=...  12.2 us
    dot_general x1, matrix products, on_device(): jnp.einsum('nij,njr->nir', ratio, gene_tiles, preferred_element_type=jnp....  11.7 us
    dot_general x1, matrix products, on_device(): jnp.einsum('bn,nir->bir', row_pick, terms, precision=lax.Precision.HIGHEST)  8.37 us
    dot_general x1, matrix products, on_device(): jnp.einsum('bn,njr->bjr', col_pick, terms_next, precision=lax.Precision.H...  8.16 us
  transfers between devices with their start and end apart: 3, of which 3 were waited for; matrix products, arithmetic and copies ran while one was open for 2% of the time, Pallas kernels for 0%

commit v1 on v0

--- a/solution.py
+++ b/solution.py
@@ -33,7 +33,10 @@
     numer = jnp.einsum("bn,nir->bir", row_pick, terms, precision=lax.Precision.HIGHEST).reshape(
         -1, rank
     )
-    whole = lax.psum(numer, "gene")
+    size, whole = (lax.axis_size("gene"), numer)
+    for far in [1 << k for k in range(size.bit_length() - 1)]:
+        route = [(i, i ^ far) for i in range(size)]
+        whole = whole + lax.ppermute(whole, "gene", route)
     group_new = cell_full * whole / gene_totals
     new_bf = group_new.astype(jnp.bfloat16)
     cell_sums = lax.psum(jnp.sum(group_new, 0), "cell")

time: 242 us -> 352 us (1.45)
  blocking collectives: 36.8 us -> 104 us
  waiting for transfers between devices: 129 us -> 171 us
    ppermute x0 -> x4, waiting for transfers between devices: none -> 97.7 us  [on_device(): whole = whole + lax.ppermute(whole, 'gene', route)]
    psum x1, blocking collectives: 31.9 us -> 98.9 us  [on_device(): gene_totals = lax.psum(jnp.sum(gene_factor, 0), 'gene')]
    psum x1 -> x0, waiting for transfers between devices: 65.2 us -> none  [on_device(): whole = lax.psum(numer, 'gene')]
    psum x1, waiting for transfers between devices: 22.5 us -> 31.3 us  [on_device(): total = lax.psum(numer_gene, 'cell')]
  transfers between devices with their start and end apart: 3 -> 6, of which waited for: 3 -> 5; matrix products, arithmetic and copies ran while one was open for 2% -> 2% of each run, Pallas kernels for 0% -> 0%
where the time goes in v1:
time: 352 us
  waiting for transfers between devices  171 us (49%)
  blocking collectives  104 us (30%)
  matrix products  40.5 us (12%)
  between operations  14.8 us (4%)
  local copies, waits for them, and re-layouts  10.3 us (3%)
  other arithmetic  9.85 us (3%)
    psum x1, blocking collectives, on_device(): gene_totals = lax.psum(jnp.sum(gene_factor, 0), 'gene')  98.9 us
    ppermute x4, waiting for transfers between devices, on_device(): whole = whole + lax.ppermute(whole, 'gene', route)  97.7 us
    all_gather x1, waiting for transfers between devices, on_device(): cell_full = lax.all_gather(cell_factor, 'gene', axis=0, tiled=True)  40.9 us
    psum x1, waiting for transfers between devices, on_device(): total = lax.psum(numer_gene, 'cell')  31.3 us
    dot_general x1, matrix products, on_device(): jnp.einsum('nij,nir->njr', ratio_next, new_tiles, preferred_element_type=...  12.2 us
    dot_general x1, matrix products, on_device(): jnp.einsum('nij,njr->nir', ratio, gene_tiles, preferred_element_type=jnp....  11.7 us
    dot_general x1, matrix products, on_device(): jnp.einsum('bn,nir->bir', row_pick, terms, precision=lax.Precision.HIGHEST)  8.37 us
    dot_general x1, matrix products, on_device(): jnp.einsum('bn,njr->bjr', col_pick, terms_next, precision=lax.Precision.H...  8.16 us
  transfers between devices with their start and end apart: 6, of which 5 were waited for; matrix products, arithmetic and copies ran while one was open for 2% of the time, Pallas kernels for 0%

profile of v1, /device:TPU:0, one launch (start us, length us, event | category | flops | bytes accessed | tf_op | source)
XLA Modules:
  0.0 352.0 jit_solution(16150226813427497031)
XLA Ops:
  7.2 0.7 all-gather.2.cloned.1.call-update
  9.3 1.4 fusion.23
  10.7 2.7 gather_fusion.1
  13.4 40.9 %all-gather.2.cloned.1.call-done = f32[4096,128]{1,0:T(8,128)} async-done(((f32[256,128]{1,0:T(8,128)}), f32[4096,128]{1,0:T(8,128)}) %all-gather.2.cloned.1.call-update) | async-done | bytes 2097168 | tf_op jit(solution)/shard_map/all_gather | solution.py:21
  54.3 1.7 convert_element_type.29
  56.0 2.7 gather_fusion
  58.7 11.7 %fusion.10 = f32[48,256,128]{2,1,0:T(8,128)} fusion(bf16[48,256,128]{2,1,0:T(8,128)(2,1)} %gather_fusion.1, bf16[48,256,256]{2,1,0:T(8,128)(2,1)} %param.6, f32[48]{0:T(128)S(1)} %compare_convert_fusion, bf16[48,256,128]{2,1,0:T(8,128)(2,1)} %gather_fusion), kind=kOutput, calls=%fused_computation.14 | convolution fusion | flops 1623195648 | bytes 18874560 | tf_op jit(solution)/shard_map/nij,njr->nir/dot_general | solution.py:32
  70.4 8.4 %fusion.6 = f32[16,256,128]{2,0,1:T(8,128)S(1)} fusion(f32[48,256,128]{2,1,0:T(8,128)} %fusion.10, s32[48]{0:T(128)S(1)} %copy-done.2), kind=kOutput, calls=%fused_computation.11 | convolution fusion | flops 301990656 | bytes 8388800 | tf_op jit(solution)/shard_map/bn,nir->bir/dot_general | solution.py:33
  78.8 0.7 copy.8
  79.8 3.9 %collective-permute-done = f32[4096,128]{1,0:T(8,128)S(1)} collective-permute-done((f32[4096,128]{1,0:T(8,128)S(1)}, f32[4096,128]{1,0:T(8,128)S(1)}, u32[]{:S(2)}, u32[]{:S(2)}) %collective-permute-start) | collective-permute-done | bytes 2097184 | tf_op jit(solution)/shard_map/ppermute | solution.py:39
  83.9 0.7 collective-permute-start.1
  84.6 47.2 %collective-permute-done.1 = f32[4096,128]{1,0:T(8,128)S(1)} collective-permute-done((f32[4096,128]{1,0:T(8,128)S(1)}, f32[4096,128]{1,0:T(8,128)S(1)}, u32[]{:S(2)}, u32[]{:S(2)}) %collective-permute-start.1) | collective-permute-done | bytes 2097184 | tf_op jit(solution)/shard_map/ppermute | solution.py:39
  132.4 46.6 %collective-permute-done.2 = f32[4096,128]{1,0:T(8,128)S(1)} collective-permute-done((f32[4096,128]{1,0:T(8,128)S(1)}, f32[4096,128]{1,0:T(8,128)S(1)}, u32[]{:S(2)}, u32[]{:S(2)}) %collective-permute-start.2) | collective-permute-done | bytes 2097184 | tf_op jit(solution)/shard_map/ppermute | solution.py:39
  179.2 0.9 collective-permute-start.3
  180.1 98.9 %psum.21 = f32[128]{0:T(128)S(1)} all-reduce(f32[128]{0:T(128)S(1)} %get-tuple-element.5), channel_id=1, replica_groups=mesh['cell'=2,'gene'=16] {'gene'}, use_global_device_ids=true, to_apply=%region_1.0 | all-reduce | flops 128 | bytes 1024 | tf_op jit(solution)/shard_map/psum | solution.py:20
  279.0 3.4 fusion.22
  282.5 2.7 gather_fusion.2
  285.2 12.2 %fusion.8 = f32[48,256,128]{2,1,0:T(8,128)} fusion(bf16[48,256,128]{2,1,0:T(8,128)(2,1)} %gather_fusion.2, bf16[48,256,256]{2,1,0:T(8,128)(2,1)} %param.6, f32[48]{0:T(128)S(1)} %compare_convert_fusion, bf16[48,256,128]{2,1,0:T(8,128)(2,1)} %gather_fusion.1), kind=kOutput, calls=%fused_computation.13 | convolution fusion | flops 1623195648 | bytes 18874560 | tf_op jit(solution)/shard_map/nij,nir->njr/dot_general | solution.py:47
  297.4 8.2 %fusion.4 = f32[4,256,128]{2,0,1:T(4,128)S(1)} fusion(f32[48,256,128]{2,1,0:T(8,128)} %fusion.8, s32[48]{0:T(128)S(1)} %copy-done.3), kind=kOutput, calls=%fused_computation.9 | convolution fusion | flops 75497664 | bytes 6815936 | tf_op jit(solution)/shard_map/bn,njr->bjr/dot_general | solution.py:50
  305.6 0.8 copy.9
  306.5 4.9 %psum.23 = f32[128]{0:T(128)S(1)} all-reduce(f32[128]{0:T(128)S(1)} %get-tuple-element.2), channel_id=1, replica_groups=mesh['cell'=2,'gene'=16] {'cell'}, use_global_device_ids=true, to_apply=%region_4.0 | all-reduce | flops 128 | bytes 1024 | tf_op jit(solution)/shard_map/psum | solution.py:42
  311.4 0.7 constant_dynamic-slice_fusion
  312.1 31.3 %all-reduce.2.cloned.1.call-done = f32[1024,128]{1,0:T(8,128)} async-done(((f32[1024,128]{1,0:T(8,128)}), f32[1024,128]{1,0:T(8,128)}) %all-reduce.2.cloned.1.call-update) | async-done | bytes 524304 | tf_op jit(solution)/shard_map/psum | solution.py:53
  343.3 1.9 multiply_divide_fusion.1
  (23 shorter events, 2.2 us)
Async XLA Ops:
  7.2 47.2 %all-gather.2.cloned.1.call-start = ((), (), s32[]{:S(2)}) async-start(), calls=%async_computation | async-start | bytes 2228224 | tf_op jit(solution)/shard_map/all_gather | solution.py:21
  7.9 335.4 %all-reduce.2.cloned.1.call-start = ((), (), s32[]{:S(2)}) async-start(), calls=%async_computation.1 | async-start | bytes 1048576 | tf_op jit(solution)/shard_map/psum | solution.py:53
  10.7 2.8 copy-start.2
  79.5 4.2 %collective-permute-start = (f32[4096,128]{1,0:T(8,128)S(1)}, f32[4096,128]{1,0:T(8,128)S(1)}, u32[]{:S(2)}, u32[]{:S(2)}) collective-permute-start(f32[4096,128]{1,0:T(8,128)S(1)} %bitcast.23), channel_id=1, source_target_pairs={{0,1},{1,0},{2,3},{3,2},{4,5},{5,4},{6,7},{7,6},{8,9},{9,8},{10,11... | collective-permute-start | bytes 6291464 | tf_op jit(solution)/shard_map/ppermute | solution.py:39
  83.9 47.8 %collective-permute-start.1 = (f32[4096,128]{1,0:T(8,128)S(1)}, f32[4096,128]{1,0:T(8,128)S(1)}, u32[]{:S(2)}, u32[]{:S(2)}) collective-permute-start(f32[4096,128]{1,0:T(8,128)S(1)} %bitcast_add_fusion), channel_id=1, source_target_pairs={{0,2},{1,3},{2,0},{3,1},{4,6},{5,7},{6,4},{7,5},{8,10},{9,11},{10,... | collective-permute-start | bytes 6291464 | tf_op jit(solution)/shard_map/ppermute | solution.py:39
  132.0 47.0 %collective-permute-start.2 = (f32[4096,128]{1,0:T(8,128)S(1)}, f32[4096,128]{1,0:T(8,128)S(1)}, u32[]{:S(2)}, u32[]{:S(2)}) collective-permute-start(f32[4096,128]{1,0:T(8,128)S(1)} %add.35), channel_id=1, source_target_pairs={{0,4},{1,5},{2,6},{3,7},{4,0},{5,1},{6,2},{7,3},{8,12},{9,13},{10,... | collective-permute-start | bytes 6291464 | tf_op jit(solution)/shard_map/ppermute | solution.py:39
  179.2 99.8 %copy-start = (f32[4096,128]{1,0:T(8,128)}, f32[4096,128]{1,0:T(8,128)S(1)}, u32[]{:S(2)}) copy-start(f32[4096,128]{1,0:T(8,128)S(1)} %add.36) | copy-start | bytes 6291460
  179.2 99.8 %collective-permute-start.3 = (f32[4096,128]{1,0:T(8,128)S(1)}, f32[4096,128]{1,0:T(8,128)}, u32[]{:S(2)}, u32[]{:S(2)}) collective-permute-start(f32[4096,128]{1,0:T(8,128)S(1)} %add.36), channel_id=1, source_target_pairs={{0,8},{1,9},{2,10},{3,11},{4,12},{5,13},{6,14},{7,15},{8,0},{9,1},... | collective-permute-start | bytes 6291464 | tf_op jit(solution)/shard_map/ppermute | solution.py:39
  285.2 12.2 %copy-start.3 = (s32[48]{0:T(128)S(1)}, s32[48]{0:T(128)}, u32[]{:S(2)}) copy-start(s32[48]{0:T(128)} %param.8) | copy-start | bytes 580
  297.4 45.9 %copy-start.1 = (f32[1024,128]{1,0:T(8,128)S(1)}, f32[1024,128]{1,0:T(8,128)}, u32[]{:S(2)}) copy-start(f32[1024,128]{1,0:T(8,128)} %param.11) | copy-start | bytes 1572868
Sparse Core Ops, SparseCore 0:
  10.1 44.1 all-gather.1
  306.6 36.6 all-reduce.1
